TPU v7x, 256 devices: a whole 4x4x8 slice. The times are simulated.
256 devices in a mesh: pipe: 4 (over x), seq: 64 (over y, z, core).
Axes of the slice: x: 4, y: 4, z: 8, core: 2. Of those that a mesh axis runs over, the one named last changes fastest.
Arguments:
- arriving: bfloat16 [4, 65536, 2048], P('pipe', 'seq'), may hold values from -6 to 6
- loss_grad: bfloat16 [65536, 2048], P('seq', 'pipe'), may hold values from -6 to 6
- first_blocks: bfloat16 [4, 256, 256, 256], P('pipe', 'seq'), may hold values from -0.375 to 0.375
- second_blocks: bfloat16 [4, 256, 256, 256], P('pipe', 'seq'), may hold values from -0.375 to 0.375
- inner_gain: bfloat16 [4, 2048], P('pipe'), may hold values from 0.25 to 1.75
- outer_gain: bfloat16 [4, 2048], P('pipe'), may hold values from 0.25 to 1.75
Outputs:
- entering: bfloat16 [4, 65536, 2048], P('pipe', 'seq')
- leaving: bfloat16 [65536, 2048], P('seq', 'pipe')
All inputs are finite; a program needn't handle non-finite values.
Results may differ from a plain program's by a relative error of at most 0.0059.
Values may be sent and summed in bfloat16 or wider, within the bound.
No kernel may reach another device: no remote copies, remote signals or barrier semaphores. Data moves between devices by JAX's collectives and lax.ppermute only.
A program may use at most 128 MiB of HBM per device.

v0:
```python
import jax
import jax.numpy as jnp
from jax import lax
from jax.sharding import PartitionSpec as P


def shifted(block, axis, distance):
    devices = range(lax.axis_size(axis))
    route = [((i - distance) % len(devices), i) for i in devices]
    return lax.ppermute(block, axis, route)


def from_root(array, axis, root):
    mine = lax.axis_index(axis) == root
    return lax.psum(jnp.where(mine, array, jnp.zeros_like(array)), axis)


def mixer(gradient, first_part, second_part, inner_part, outer_part):
    row_count = first_part.shape[0]
    block_order = first_part.shape[1]
    blocked = gradient.reshape(row_count, block_order, gradient.shape[1]).astype(jnp.float32)
    scaled = (blocked * inner_part.astype(jnp.float32)).astype(jnp.bfloat16)
    mixed = jnp.einsum(
        "kjc,jki->ijc",
        lax.all_to_all(scaled, "seq", split_axis=1, concat_axis=0, tiled=True),
        second_part,
        preferred_element_type=jnp.float32,
    ).astype(jnp.bfloat16)
    returned = lax.all_to_all(mixed, "seq", split_axis=0, concat_axis=1, tiled=True)
    spread = jnp.einsum("ikc,ikj->ijc", returned, first_part, preferred_element_type=jnp.float32)
    result = blocked + outer_part.astype(jnp.float32) * spread
    return result.astype(jnp.bfloat16).reshape(gradient.shape)


def per_device(arriving, loss_grad, first_blocks, second_blocks, inner_gain, outer_gain):
    sections = lax.axis_size("pipe")
    position = lax.axis_index("pipe")
    whole_loss = lax.all_gather(loss_grad, "pipe", axis=1, tiled=True)
    own_result = mixer(arriving[0], first_blocks[0], second_blocks[0], inner_gain[0], outer_gain[0])
    passed = shifted(own_result, "pipe", -1)
    exit_root = sections - 1
    source = jnp.where(position == sections - 1, whole_loss, passed)
    entering = mixer(source, first_blocks[0], second_blocks[0], inner_gain[0], outer_gain[0])
    copied = from_root(passed, "pipe", exit_root)
    channel_width = loss_grad.shape[1]
    leaving = lax.dynamic_slice_in_dim(copied, position * channel_width, channel_width, 1)
    return (entering[None], leaving)


def solution(mesh):
    placed = (
        P("pipe", "seq", None),
        P("seq", "pipe"),
        P("pipe", "seq", None, None),
        P("pipe", "seq", None, None),
        P("pipe", None),
        P("pipe", None),
    )
    return jax.shard_map(
        per_device,
        mesh=mesh,
        in_specs=placed,
        out_specs=(P("pipe", "seq", None), P("seq", "pipe")),
        check_vma=False,
    )
```

profile of v0, /device:TPU:1, one launch (start us, length us, event | category | flops | bytes accessed | tf_op | source)
XLA Modules:
  0.0 639.2 jit_solution(10214228244827802752)
XLA Ops:
  7.2 0.0 copy-start
  7.2 0.8 convert_element_type.76
  7.9 3.3 fusion
  11.2 3.2 copy.24
  14.5 109.1 %all_to_all.72 = bf16[4,256,2048]{2,0,1:T(4,128)(2,1)S(1)} all-to-all(bf16[4,256,2048]{2,0,1:T(4,128)(2,1)S(1)} %copy.24), channel_id=1, replica_groups=mesh['pipe'=4,'seq'=64] {'seq'}, dimensions={1} | all-to-all | bytes 8388608 | tf_op jit(solution)/shard_map/all_to_all | solution.py:25
  123.6 8.3 %copy.25 = bf16[4,64,4,2048]{3,2,0,1:T(4,128)(2,1)S(1)} copy(bf16[4,64,4,2048]{3,0,2,1:T(4,128)(2,1)S(1)} %bitcast.44) | data formatting | bytes 8388608 | tf_op jit(solution)/shard_map/all_to_all | solution.py:25
  131.9 0.0 copy-done
  131.9 7.7 %convert_bitcast_fusion.1 = bf16[256,4,2048]{0,2,1:T(8,128)(2,1)} fusion(bf16[256,4,2048]{2,1,0:T(4,128)(2,1)S(1)} %bitcast.45, bf16[1,4,256,256]{3,2,1,0:T(8,128)(2,1)S(1)} %copy-done), kind=kOutput, calls=%fused_computation.13 | convolution fusion | flops 1075838976 | bytes 8912896 | tf_op jit(solution)/shard_map/kjc,jki->ijc/dot_general | solution.py:23
  139.6 7.9 %copy.27 = bf16[256,4,2048]{2,1,0:T(4,128)(2,1)} copy(bf16[256,4,2048]{0,2,1:T(8,128)(2,1)} %convert_bitcast_fusion.1) | data formatting | bytes 8388608 | tf_op jit(solution)/shard_map/convert_element_type | solution.py:28
  147.5 0.0 copy-start.3
  147.5 6.2 all-to-all-start.1
  153.7 0.0 all-gather.2.cloned.1.call-start
  153.7 0.7 all-gather.2.cloned.1.call-update
  154.4 0.0 copy-done.3
  154.4 95.1 %all-to-all-done.1 = bf16[256,4,2048]{2,1,0:T(4,128)(2,1)} async-done(((bf16[256,4,2048]{2,1,0:T(4,128)(2,1)}), bf16[256,4,2048]{2,1,0:T(4,128)(2,1)}, u32[]{:S(2)}, u32[]{:S(2)}) %all-to-all-start.1) | async-done | bytes 4194336 | tf_op jit(solution)/shard_map/all_to_all | solution.py:29
  249.5 7.0 %copy.28 = bf16[4,64,4,2048]{3,2,1,0:T(4,128)(2,1)} copy(bf16[4,64,4,2048]{3,2,0,1:T(4,128)(2,1)} %bitcast.10) | data formatting | bytes 8388608 | tf_op jit(solution)/shard_map/all_to_all | solution.py:29
  256.5 0.0 copy-start.2
  256.5 7.0 %all_to_all.59 = bf16[4,256,2048]{2,1,0:T(8,128)(2,1)} reshape(bf16[4,64,4,2048]{3,2,1,0:T(4,128)(2,1)} %copy.28) | data formatting | bytes 8388608 | tf_op jit(solution)/shard_map/all_to_all | solution.py:29
  263.5 0.0 copy-done.2
  263.5 6.9 %fusion.1 = bf16[4,256,2048]{2,1,0:T(8,128)(2,1)} fusion(bf16[4,256,2048]{2,1,0:T(8,128)(2,1)} %bitcast.49, bf16[4,256,2048]{2,1,0:T(8,128)(2,1)} %all_to_all.59, f32[2048]{0:T(1024)S(1)} %bitcast.53, bf16[1,4,256,256]{3,2,1,0:T(8,128)(2,1)S(1)} %copy-done.2), kind=kOutput, calls=%fused_computation.5 | convolution fusion | flops 1082130432 | bytes 13115392 | tf_op jit(solution)/shard_map/ikc,ikj->ijc/dot_general | solution.py:30
  270.5 2.5 collective-permute-start
  272.9 0.0 all-gather.2.cloned.1.call-done
  273.0 90.0 %collective-permute-done = bf16[1024,2048]{1,0:T(8,128)(2,1)} collective-permute-done((bf16[1024,2048]{1,0:T(8,128)(2,1)}, bf16[1024,2048]{1,0:T(8,128)(2,1)}, u32[]{:S(2)}, u32[]{:S(2)}) %collective-permute-start) | collective-permute-done | bytes 4194336 | tf_op jit(solution)/shard_map/ppermute | solution.py:10
  362.9 3.9 broadcast_select_fusion
  366.8 0.0 copy-start.1
  366.8 1.9 copy-done.1
  368.8 1.2 fusion.2
  369.9 3.2 copy.30
  373.2 101.9 %all_to_all.73 = bf16[4,256,2048]{2,0,1:T(4,128)(2,1)S(1)} all-to-all(bf16[4,256,2048]{2,0,1:T(4,128)(2,1)S(1)} %copy.30), channel_id=1, replica_groups=mesh['pipe'=4,'seq'=64] {'seq'}, dimensions={1} | all-to-all | bytes 8388608 | tf_op jit(solution)/shard_map/all_to_all | solution.py:25
  475.1 8.3 %copy.31 = bf16[4,64,4,2048]{3,2,0,1:T(4,128)(2,1)S(1)} copy(bf16[4,64,4,2048]{3,0,2,1:T(4,128)(2,1)S(1)} %bitcast.46) | data formatting | bytes 8388608 | tf_op jit(solution)/shard_map/all_to_all | solution.py:25
  483.4 7.5 %convert_bitcast_fusion = bf16[256,4,2048]{0,2,1:T(8,128)(2,1)} fusion(bf16[256,4,2048]{2,1,0:T(4,128)(2,1)S(1)} %bitcast.47, bf16[1,4,256,256]{3,2,1,0:T(8,128)(2,1)S(1)} %copy-done), kind=kOutput, calls=%fused_computation.12 | convolution fusion | flops 1075838976 | bytes 8912896 | tf_op jit(solution)/shard_map/kjc,jki->ijc/dot_general | solution.py:23
  490.8 8.0 %copy.33 = bf16[256,4,2048]{2,1,0:T(4,128)(2,1)} copy(bf16[256,4,2048]{0,2,1:T(8,128)(2,1)} %convert_bitcast_fusion) | data formatting | bytes 8388608 | tf_op jit(solution)/shard_map/convert_element_type | solution.py:28
  498.8 6.0 all-to-all-start.3
  504.8 0.0 all-reduce.2.cloned.1.call-start
  504.9 0.7 all-reduce.2.cloned.1.call-update
  505.6 103.4 %all-reduce.2.cloned.1.call-done = bf16[1024,2048]{1,0:T(8,128)(2,1)} async-done(((bf16[1024,2048]{1,0:T(8,128)(2,1)}), bf16[1024,2048]{1,0:T(8,128)(2,1)}) %all-reduce.2.cloned.1.call-update) | async-done | bytes 4194320 | tf_op jit(solution)/shard_map/psum | solution.py:15
  609.0 2.3 constant_dynamic-slice_fusion
  611.2 0.0 all-to-all-done.3
  611.2 7.0 %copy.34 = bf16[4,64,4,2048]{3,2,1,0:T(4,128)(2,1)} copy(bf16[4,64,4,2048]{3,2,0,1:T(4,128)(2,1)} %bitcast.21) | data formatting | bytes 8388608 | tf_op jit(solution)/shard_map/all_to_all | solution.py:29
  618.2 6.9 %all_to_all.67 = bf16[4,256,2048]{2,1,0:T(8,128)(2,1)} reshape(bf16[4,64,4,2048]{3,2,1,0:T(4,128)(2,1)} %copy.34) | data formatting | bytes 8388608 | tf_op jit(solution)/shard_map/all_to_all | solution.py:29
  625.2 6.9 %fusion.3 = bf16[4,256,2048]{2,1,0:T(8,128)(2,1)} fusion(bf16[4,256,2048]{2,1,0:T(8,128)(2,1)} %bitcast.43, bf16[4,256,2048]{2,1,0:T(8,128)(2,1)} %all_to_all.67, f32[2048]{0:T(1024)S(1)} %bitcast.54, bf16[1,4,256,256]{3,2,1,0:T(8,128)(2,1)S(1)} %copy-done.2), kind=kOutput, calls=%fused_computation.7 | convolution fusion | flops 1082130432 | bytes 13115392 | tf_op jit(solution)/shard_map/ikc,ikj->ijc/dot_general | solution.py:30
  (1 shorter events, 0.0 us)
Async XLA Ops:
  7.2 124.7 %copy-start = (bf16[1,4,256,256]{3,2,1,0:T(8,128)(2,1)S(1)}, bf16[1,4,256,256]{3,2,1,0:T(8,128)(2,1)}, u32[]{:S(2)}) copy-start(bf16[1,4,256,256]{3,2,1,0:T(8,128)(2,1)} %param.9) | copy-start | bytes 1572868
  147.5 6.9 %copy-start.3 = (bf16[1,2048]{1,0:T(2,128)(2,1)S(1)}, bf16[1,2048]{1,0:T(2,128)(2,1)}, u32[]{:S(2)}) copy-start(bf16[1,2048]{1,0:T(2,128)(2,1)} %param.11) | copy-start | bytes 12292
  147.5 102.0 %all-to-all-start.1 = ((bf16[256,4,2048]{2,1,0:T(4,128)(2,1)}), bf16[256,4,2048]{2,1,0:T(4,128)(2,1)}, u32[]{:S(2)}, u32[]{:S(2)}) async-start(bf16[256,4,2048]{2,1,0:T(4,128)(2,1)} %copy.27), calls=%async_computation.1 | async-start | bytes 8388608 | tf_op jit(solution)/shard_map/all_to_all | solution.py:29
  153.7 119.3 %all-gather.2.cloned.1.call-start = ((), (), s32[]{:S(2)}) async-start(), calls=%async_computation.4 | async-start | bytes 5242880 | tf_op jit(solution)/shard_map/all_gather | solution.py:38
  256.5 7.0 %copy-start.2 = (bf16[1,4,256,256]{3,2,1,0:T(8,128)(2,1)S(1)}, bf16[1,4,256,256]{3,2,1,0:T(8,128)(2,1)}, u32[]{:S(2)}) copy-start(bf16[1,4,256,256]{3,2,1,0:T(8,128)(2,1)} %param.8) | copy-start | bytes 1572868
  270.5 92.5 %collective-permute-start = (bf16[1024,2048]{1,0:T(8,128)(2,1)}, bf16[1024,2048]{1,0:T(8,128)(2,1)}, u32[]{:S(2)}, u32[]{:S(2)}) collective-permute-start(bf16[1024,2048]{1,0:T(8,128)(2,1)} %bitcast.13), channel_id=1, source_target_pairs={{64,0},{128,64},{192,128},{0,192},{65,1},{129,65},{193,129},{1,193... | collective-permute-start | bytes 12582920 | tf_op jit(solution)/shard_map/ppermute | solution.py:10
  366.8 1.9 copy-start.1
  498.8 112.4 %all-to-all-start.3 = ((bf16[256,4,2048]{2,1,0:T(4,128)(2,1)}), bf16[256,4,2048]{2,1,0:T(4,128)(2,1)}, u32[]{:S(2)}, u32[]{:S(2)}) async-start(bf16[256,4,2048]{2,1,0:T(4,128)(2,1)} %copy.33), calls=%async_computation.3 | async-start | bytes 8388608 | tf_op jit(solution)/shard_map/all_to_all | solution.py:29
  504.8 104.1 %all-reduce.2.cloned.1.call-start = ((), (), s32[]{:S(2)}) async-start(), calls=%async_computation.5 | async-start | bytes 8388608 | tf_op jit(solution)/shard_map/psum | solution.py:15
Sparse Core Ops, SparseCore 0:
  156.3 51.5 all-gather.1
  508.6 100.3 all-reduce.1
where the time goes:
time: 645 us; the launch traced here: 639 us
  waiting for transfers between devices  290 us (45%)
  blocking collectives  211 us (33%)
  local copies, waits for them, and re-layouts  71.2 us (11%)
  matrix products  29 us (4%)
  starting transfers between devices  14.7 us (2%)
  between operations  14.4 us (2%)
  other arithmetic  9.1 us (1%)
    all_to_all x2, blocking collectives, mixer(): lax.all_to_all(scaled, 'seq', split_axis=1, concat_axis=0, tiled=True)  211 us
    psum x1, waiting for transfers between devices, from_root(): return lax.psum(jnp.where(mine, array, jnp.zeros_like(array)), axis)  103 us
    all_to_all x2, waiting for transfers between devices, mixer(): lax.all_to_all(mixed, 'seq', split_axis=0, concat_axis=1, tiled=True)  95.1 us
    ppermute x1, waiting for transfers between devices, shifted(): return lax.ppermute(block, axis, route)  90 us
    all_to_all x4, local copies, waits for them, and re-layouts, mixer(): lax.all_to_all(mixed, 'seq', split_axis=0, concat_axis=1, tiled=True)  27.9 us
    all_to_all x2, local copies, waits for them, and re-layouts, mixer(): lax.all_to_all(scaled, 'seq', split_axis=1, concat_axis=0, tiled=True)  16.6 us
    convert_element_type x2, local copies, waits for them, and re-layouts, mixer(): mixed = jnp.einsum('kjc,jki->ijc', lax.all_to_all(scaled, 'seq', split_ax...  15.9 us
    dot_general x2, matrix products, mixer(): jnp.einsum('kjc,jki->ijc', lax.all_to_all(scaled, 'seq', split_axis=1, co...  15.2 us
  transfers between devices with their start and end apart: 5, of which 3 were waited for; matrix products, arithmetic and copies ran while one was open for 3% of the time, Pallas kernels for 0%

commit v1 on v0

--- a/solution.py
+++ b/solution.py
@@ -2,6 +2,16 @@
 import jax.numpy as jnp
 from jax import lax
 from jax.sharding import PartitionSpec as P
+
+change_counts = lambda panel: jnp.concatenate(
+    jax.lax.all_to_all(
+        jnp.stack(jnp.split(panel, jax.lax.psum(1, axis_name="seq"), axis=1)),
+        axis_name="seq",
+        split_axis=0,
+        concat_axis=0,
+    ),
+    0,
+)
 
 
 def shifted(block, axis, distance):
@@ -21,10 +31,7 @@
     blocked = gradient.reshape(row_count, block_order, gradient.shape[1]).astype(jnp.float32)
     scaled = (blocked * inner_part.astype(jnp.float32)).astype(jnp.bfloat16)
     mixed = jnp.einsum(
-        "kjc,jki->ijc",
-        lax.all_to_all(scaled, "seq", split_axis=1, concat_axis=0, tiled=True),
-        second_part,
-        preferred_element_type=jnp.float32,
+        "kjc,jki->ijc", change_counts(scaled), second_part, preferred_element_type=jnp.float32
     ).astype(jnp.bfloat16)
     returned = lax.all_to_all(mixed, "seq", split_axis=0, concat_axis=1, tiled=True)
     spread = jnp.einsum("ikc,ikj->ijc", returned, first_part, preferred_element_type=jnp.float32)

time: 645 us -> 621 us (0.963)
  local copies, waits for them, and re-layouts: 71.2 us -> 52.4 us
    all_to_all x2 -> x0, local copies, waits for them, and re-layouts: 16.6 us -> none  [mixer(): lax.all_to_all(scaled, 'seq', split_axis=1, concat_axis=0, tiled=True)]
    convert_element_type x4 -> x2, local copies, waits for them, and re-layouts: 22.4 us -> 15.9 us  [mixer(): mixed = jnp.einsum('kjc,jki->ijc', change_counts(scaled), second_part, pr...]
where the time goes in v1:
time: 621 us; the launch traced here: 620 us
  waiting for transfers between devices  290 us (47%)
  blocking collectives  211 us (34%)
  local copies, waits for them, and re-layouts  52.4 us (8%)
  matrix products  28.2 us (5%)
  starting transfers between devices  14.9 us (2%)
  between operations  14.2 us (2%)
  other arithmetic  9.3 us (1%)
    all_to_all x2, blocking collectives, jax.lax.all_to_all(jnp.stack(jnp.split(panel, jax.lax.psum(1, axis_name='...  211 us
    psum x1, waiting for transfers between devices, from_root(): return lax.psum(jnp.where(mine, array, jnp.zeros_like(array)), axis)  103 us
    all_to_all x2, waiting for transfers between devices, mixer(): lax.all_to_all(mixed, 'seq', split_axis=0, concat_axis=1, tiled=True)  95.1 us
    ppermute x1, waiting for transfers between devices, shifted(): return lax.ppermute(block, axis, route)  90 us
    all_to_all x4, local copies, waits for them, and re-layouts, mixer(): lax.all_to_all(mixed, 'seq', split_axis=0, concat_axis=1, tiled=True)  27.9 us
    convert_element_type x2, local copies, waits for them, and re-layouts, mixer(): mixed = jnp.einsum('kjc,jki->ijc', change_counts(scaled), second_part, pr...  15.9 us
    dot_general x2, matrix products, mixer(): jnp.einsum('kjc,jki->ijc', change_counts(scaled), second_part, preferred_...  14.3 us
    dot_general x2, matrix products, mixer(): jnp.einsum('ikc,ikj->ijc', returned, first_part, preferred_element_type=j...  13.9 us
  transfers between devices with their start and end apart: 5, of which 3 were waited for; matrix products, arithmetic and copies ran while one was open for 3% of the time, Pallas kernels for 0%

profile of v1, /device:TPU:1, one launch (start us, length us, event | category | flops | bytes accessed | tf_op | source)
XLA Modules:
  0.0 619.6 jit_solution(5609641419897925825)
XLA Ops:
  7.2 0.8 convert_element_type.76
  7.9 3.3 fusion
  11.3 0.1 constant_dynamic-update-slice_fusion.62
  11.4 0.1 constant_dynamic-update-slice_fusion.60
  11.4 0.1 constant_dynamic-update-slice_fusion.58
  11.5 0.1 constant_dynamic-update-slice_fusion.56
  11.6 0.1 constant_dynamic-update-slice_fusion.54
  11.7 0.1 constant_dynamic-update-slice_fusion.52
  11.8 0.1 constant_dynamic-update-slice_fusion.50
  11.9 0.1 constant_dynamic-update-slice_fusion.48
  12.0 0.1 constant_dynamic-update-slice_fusion.46
  12.0 0.1 constant_dynamic-update-slice_fusion.44
  12.1 0.1 constant_dynamic-update-slice_fusion.42
  12.2 0.1 constant_dynamic-update-slice_fusion.40
  12.3 0.1 constant_dynamic-update-slice_fusion.38
  12.4 0.1 constant_dynamic-update-slice_fusion.36
  12.5 0.1 constant_dynamic-update-slice_fusion.34
  12.6 0.1 constant_dynamic-update-slice_fusion.32
  12.6 0.1 constant_dynamic-update-slice_fusion.30
  12.7 0.1 constant_dynamic-update-slice_fusion.28
  12.8 0.1 constant_dynamic-update-slice_fusion.26
  12.9 0.1 constant_dynamic-update-slice_fusion.24
  13.0 0.1 constant_dynamic-update-slice_fusion.22
  13.1 0.1 constant_dynamic-update-slice_fusion.20
  13.1 0.1 constant_dynamic-update-slice_fusion.18
  13.2 0.1 constant_dynamic-update-slice_fusion.16
  13.3 0.1 constant_dynamic-update-slice_fusion.14
  13.4 0.1 constant_dynamic-update-slice_fusion.12
  13.5 0.1 constant_dynamic-update-slice_fusion.10
  13.6 0.1 constant_dynamic-update-slice_fusion.8
  13.7 0.1 constant_dynamic-update-slice_fusion.6
  13.7 0.1 constant_dynamic-update-slice_fusion.4
  13.8 0.1 constant_dynamic-update-slice_fusion.2
  13.9 0.1 constant_dynamic-update-slice_fusion
  14.0 109.1 %all_to_all.46 = bf16[64,4,4,2048]{3,2,1,0:T(4,128)(2,1)S(1)} all-to-all(bf16[64,4,4,2048]{3,2,1,0:T(4,128)(2,1)S(1)} %constant_dynamic-update-slice_fusion), channel_id=1, replica_groups=mesh['pipe'=4,'seq'=64] {'seq'}, dimensions={0} | all-to-all | bytes 8388608 | tf_op jit(solution)/shard_map/all_to_all | solution.py:7
  123.1 7.2 %convert_bitcast_fusion.1 = bf16[256,4,2048]{0,2,1:T(8,128)(2,1)} fusion(bf16[256,4,2048]{2,1,0:T(4,128)(2,1)S(1)} %bitcast.550, bf16[1,4,256,256]{3,2,1,0:T(8,128)(2,1)S(1)} %copy-done), kind=kOutput, calls=%fused_computation.13 | convolution fusion | flops 1075838976 | bytes 8912896 | tf_op jit(solution)/shard_map/kjc,jki->ijc/dot_general | solution.py:33
  130.2 7.9 %copy.23 = bf16[256,4,2048]{2,1,0:T(4,128)(2,1)} copy(bf16[256,4,2048]{0,2,1:T(8,128)(2,1)} %convert_bitcast_fusion.1) | data formatting | bytes 8388608 | tf_op jit(solution)/shard_map/convert_element_type | solution.py:35
  138.2 6.2 all-to-all-start.1
  144.3 0.2 all-gather.2.cloned.1.call-start
  144.5 0.5 all-gather.2.cloned.1.call-update
  145.1 95.1 %all-to-all-done.1 = bf16[256,4,2048]{2,1,0:T(4,128)(2,1)} async-done(((bf16[256,4,2048]{2,1,0:T(4,128)(2,1)}), bf16[256,4,2048]{2,1,0:T(4,128)(2,1)}, u32[]{:S(2)}, u32[]{:S(2)}) %all-to-all-start.1) | async-done | bytes 4194336 | tf_op jit(solution)/shard_map/all_to_all | solution.py:36
  240.2 7.0 %copy.24 = bf16[4,64,4,2048]{3,2,1,0:T(4,128)(2,1)} copy(bf16[4,64,4,2048]{3,2,0,1:T(4,128)(2,1)} %bitcast.72) | data formatting | bytes 8388608 | tf_op jit(solution)/shard_map/all_to_all | solution.py:36
  247.2 7.0 %all_to_all.36 = bf16[4,256,2048]{2,1,0:T(8,128)(2,1)} reshape(bf16[4,64,4,2048]{3,2,1,0:T(4,128)(2,1)} %copy.24) | data formatting | bytes 8388608 | tf_op jit(solution)/shard_map/all_to_all | solution.py:36
  254.2 6.9 %fusion.1 = bf16[4,256,2048]{2,1,0:T(8,128)(2,1)} fusion(bf16[4,256,2048]{2,1,0:T(8,128)(2,1)} %bitcast.553, bf16[4,256,2048]{2,1,0:T(8,128)(2,1)} %all_to_all.36, f32[2048]{0:T(1024)S(1)} %bitcast.557, bf16[1,4,256,256]{3,2,1,0:T(8,128)(2,1)S(1)} %copy-done.2), kind=kOutput, calls=%fused_computation.5 | convolution fusion | flops 1082130432 | bytes 13115392 | tf_op jit(solution)/shard_map/ikc,ikj->ijc/dot_general | solution.py:37
  261.1 2.5 collective-permute-start
  263.6 90.0 %collective-permute-done = bf16[1024,2048]{1,0:T(8,128)(2,1)} collective-permute-done((bf16[1024,2048]{1,0:T(8,128)(2,1)}, bf16[1024,2048]{1,0:T(8,128)(2,1)}, u32[]{:S(2)}, u32[]{:S(2)}) %collective-permute-start) | collective-permute-done | bytes 4194336 | tf_op jit(solution)/shard_map/ppermute | solution.py:20
  353.6 3.9 broadcast_select_fusion
  357.5 1.4 fusion.2
  358.8 1.0 copy-done.1
  359.8 0.1 constant_dynamic-update-slice_fusion.126
  359.9 0.1 constant_dynamic-update-slice_fusion.124
  360.0 0.1 constant_dynamic-update-slice_fusion.122
  360.1 0.1 constant_dynamic-update-slice_fusion.120
  360.2 0.1 constant_dynamic-update-slice_fusion.118
  362.5 101.9 %all_to_all.47 = bf16[64,4,4,2048]{3,2,1,0:T(4,128)(2,1)S(1)} all-to-all(bf16[64,4,4,2048]{3,2,1,0:T(4,128)(2,1)S(1)} %constant_dynamic-update-slice_fusion.64), channel_id=1, replica_groups=mesh['pipe'=4,'seq'=64] {'seq'}, dimensions={0} | all-to-all | bytes 8388608 | tf_op jit(solution)/shard_map/all_to_all | solution.py:7
  464.4 7.1 %convert_bitcast_fusion = bf16[256,4,2048]{0,2,1:T(8,128)(2,1)} fusion(bf16[256,4,2048]{2,1,0:T(4,128)(2,1)S(1)} %bitcast.551, bf16[1,4,256,256]{3,2,1,0:T(8,128)(2,1)S(1)} %copy-done), kind=kOutput, calls=%fused_computation.12 | convolution fusion | flops 1075838976 | bytes 8912896 | tf_op jit(solution)/shard_map/kjc,jki->ijc/dot_general | solution.py:33
  471.5 8.0 %copy.27 = bf16[256,4,2048]{2,1,0:T(4,128)(2,1)} copy(bf16[256,4,2048]{0,2,1:T(8,128)(2,1)} %convert_bitcast_fusion) | data formatting | bytes 8388608 | tf_op jit(solution)/shard_map/convert_element_type | solution.py:35
  479.5 6.0 all-to-all-start.3
  485.6 0.7 all-reduce.2.cloned.1.call-update
  486.3 103.4 %all-reduce.2.cloned.1.call-done = bf16[1024,2048]{1,0:T(8,128)(2,1)} async-done(((bf16[1024,2048]{1,0:T(8,128)(2,1)}), bf16[1024,2048]{1,0:T(8,128)(2,1)}) %all-reduce.2.cloned.1.call-update) | async-done | bytes 4194320 | tf_op jit(solution)/shard_map/psum | solution.py:25
  589.7 2.3 constant_dynamic-slice_fusion
  591.9 7.0 %copy.28 = bf16[4,64,4,2048]{3,2,1,0:T(4,128)(2,1)} copy(bf16[4,64,4,2048]{3,2,0,1:T(4,128)(2,1)} %bitcast.145) | data formatting | bytes 8388608 | tf_op jit(solution)/shard_map/all_to_all | solution.py:36
  598.9 6.9 %all_to_all.41 = bf16[4,256,2048]{2,1,0:T(8,128)(2,1)} reshape(bf16[4,64,4,2048]{3,2,1,0:T(4,128)(2,1)} %copy.28) | data formatting | bytes 8388608 | tf_op jit(solution)/shard_map/all_to_all | solution.py:36
  605.9 6.9 %fusion.3 = bf16[4,256,2048]{2,1,0:T(8,128)(2,1)} fusion(bf16[4,256,2048]{2,1,0:T(8,128)(2,1)} %bitcast.549, bf16[4,256,2048]{2,1,0:T(8,128)(2,1)} %all_to_all.41, f32[2048]{0:T(1024)S(1)} %bitcast.558, bf16[1,4,256,256]{3,2,1,0:T(8,128)(2,1)S(1)} %copy-done.2), kind=kOutput, calls=%fused_computation.7 | convolution fusion | flops 1082130432 | bytes 13115392 | tf_op jit(solution)/shard_map/ikc,ikj->ijc/dot_general | solution.py:37
  (102 shorter events, 3.6 us)
Async XLA Ops:
  7.2 115.9 %copy-start = (bf16[1,4,256,256]{3,2,1,0:T(8,128)(2,1)S(1)}, bf16[1,4,256,256]{3,2,1,0:T(8,128)(2,1)}, u32[]{:S(2)}) copy-start(bf16[1,4,256,256]{3,2,1,0:T(8,128)(2,1)} %param.9) | copy-start | bytes 1572868
  138.2 6.9 %copy-start.3 = (bf16[1,2048]{1,0:T(2,128)(2,1)S(1)}, bf16[1,2048]{1,0:T(2,128)(2,1)}, u32[]{:S(2)}) copy-start(bf16[1,2048]{1,0:T(2,128)(2,1)} %param.11) | copy-start | bytes 12292
  138.2 102.0 %all-to-all-start.1 = ((bf16[256,4,2048]{2,1,0:T(4,128)(2,1)}), bf16[256,4,2048]{2,1,0:T(4,128)(2,1)}, u32[]{:S(2)}, u32[]{:S(2)}) async-start(bf16[256,4,2048]{2,1,0:T(4,128)(2,1)} %copy.23), calls=%async_computation.1 | async-start | bytes 8388608 | tf_op jit(solution)/shard_map/all_to_all | solution.py:36
  144.3 119.3 %all-gather.2.cloned.1.call-start = ((), (), s32[]{:S(2)}) async-start(), calls=%async_computation.4 | async-start | bytes 5242880 | tf_op jit(solution)/shard_map/all_gather | solution.py:45
  247.2 7.0 %copy-start.2 = (bf16[1,4,256,256]{3,2,1,0:T(8,128)(2,1)S(1)}, bf16[1,4,256,256]{3,2,1,0:T(8,128)(2,1)}, u32[]{:S(2)}) copy-start(bf16[1,4,256,256]{3,2,1,0:T(8,128)(2,1)} %param.8) | copy-start | bytes 1572868
  261.1 92.5 %collective-permute-start = (bf16[1024,2048]{1,0:T(8,128)(2,1)}, bf16[1024,2048]{1,0:T(8,128)(2,1)}, u32[]{:S(2)}, u32[]{:S(2)}) collective-permute-start(bf16[1024,2048]{1,0:T(8,128)(2,1)} %bitcast.75), channel_id=1, source_target_pairs={{64,0},{128,64},{192,128},{0,192},{65,1},{129,65},{193,129},{1,193... | collective-permute-start | bytes 12582920 | tf_op jit(solution)/shard_map/ppermute | solution.py:20
  357.5 2.3 copy-start.1
  479.5 112.4 %all-to-all-start.3 = ((bf16[256,4,2048]{2,1,0:T(4,128)(2,1)}), bf16[256,4,2048]{2,1,0:T(4,128)(2,1)}, u32[]{:S(2)}, u32[]{:S(2)}) async-start(bf16[256,4,2048]{2,1,0:T(4,128)(2,1)} %copy.27), calls=%async_computation.3 | async-start | bytes 8388608 | tf_op jit(solution)/shard_map/all_to_all | solution.py:36
  485.5 104.1 %all-reduce.2.cloned.1.call-start = ((), (), s32[]{:S(2)}) async-start(), calls=%async_computation.5 | async-start | bytes 8388608 | tf_op jit(solution)/shard_map/psum | solution.py:25
Sparse Core Ops, SparseCore 0:
  146.9 51.5 all-gather.1
  489.3 100.3 all-reduce.1
